TPU v7x, 512 devices: a whole 4x8x8 slice. The times are simulated.
512 devices in a mesh: node: 4 (over x), gx: 16 (over z, y_hi), gy: 8 (over y_lo, core).
Axes of the slice: x: 4, y: 8 (y_hi: 2, y_lo: 4; y = y_hi * 4 + y_lo), z: 8, core: 2. Of those that a mesh axis runs over, the one named last changes fastest.
Arguments:
- initial: float32 [5, 192, 128, 128], P(None, 'gx', 'gy'), may hold values from -8 to 50, as said below
- guesses: float32 [4, 5, 192, 128, 128], P('node', None, 'gx', 'gy'), may hold values from -8 to 50, as said below
Outputs:
- node_states: float32 [4, 5, 192, 128, 128], P('node', None, 'gx', 'gy')
Inputs may be any that keep to these rules, and one draw needn't show every extreme that they name: `initial`: each cell holds density, three momenta and total energy of a gas with ratio of heats 1.4: density 0.5 to 2.5, pressure 0.3 to 9, velocity components at most 3 in magnitude. `guesses`: each cell of each node holds density, three momenta and total energy of a gas with ratio of heats 1.4: density 0.5 to 2.5, pressure 0.3 to 9, velocity components at most 3 in magnitude.
All inputs are finite; a program needn't handle non-finite values.
Results may differ from a plain program's by a relative error of at most 0.0001.
Values sent between devices are 32-bit elements; how exact they have to be, the bound alone decides.
A program may use at most 64 MiB of HBM per device.

v0:
```python
import jax
import jax.numpy as jnp
from jax import lax
from jax.sharding import PartitionSpec as P

SWEEPS = 2


heat_ratio = 1.4
step_size = 0.025
density_floor = 0.5
pressure_floor = 0.25
epsilon = 1e-06
radau_weights = [
    [0.112999479323156, -0.040309220723522, 0.025802377420336, -0.009904676507266],
    [0.2343839957474, 0.206892573935359, -0.047857128048541, 0.016047422806516],
    [0.21668178462325, 0.406123263867373, 0.189036518170056, -0.024182104899833],
    [0.220462211176768, 0.388193468843172, 0.32884431998006, 0.0625],
]


def padded_2(cells, sides, width):
    for axis, dim in sides:
        count = lax.axis_size(axis)
        head = lax.slice_in_dim(cells, 0, width, axis=dim)
        tail = lax.slice_in_dim(cells, cells.shape[dim] - width, cells.shape[dim], axis=dim)
        cells = jnp.concatenate(
            [
                lax.ppermute(tail, axis, [(i, (i + 1) % count) for i in range(count)]),
                cells,
                lax.ppermute(head, axis, [((i + 1) % count, i) for i in range(count)]),
            ],
            axis=dim,
        )
    return cells


def primitives(fields):
    density = jnp.maximum(fields[0], density_floor)
    velocity = fields[1:4] / density
    pressure = jnp.maximum(
        0.4 * (fields[4] - 0.5 * jnp.sum(fields[1:4] * velocity, axis=0)), pressure_floor
    )
    return (density, velocity, pressure)


def local_speeds(fields):
    density, velocity, pressure = primitives(fields)
    sound = jnp.sqrt(heat_ratio * pressure / density)
    return tuple((jnp.max(jnp.abs(velocity[direction]) + sound) for direction in range(3)))


def reconstruct(first, second, third, fourth, fifth):
    cand_zero = (2.0 * first - 7.0 * second + 11.0 * third) / 6.0
    cand_one = (-second + 5.0 * third + 2.0 * fourth) / 6.0
    cand_two = (2.0 * third + 5.0 * fourth - fifth) / 6.0
    smooth_zero = (
        13.0 / 12.0 * (first - 2.0 * second + third) ** 2
        + 0.25 * (first - 4.0 * second + 3.0 * third) ** 2
    )
    smooth_one = 13.0 / 12.0 * (second - 2.0 * third + fourth) ** 2 + 0.25 * (second - fourth) ** 2
    smooth_two = (
        13.0 / 12.0 * (third - 2.0 * fourth + fifth) ** 2
        + 0.25 * (3.0 * third - 4.0 * fourth + fifth) ** 2
    )
    weight_zero = 0.1 / (epsilon + smooth_zero) ** 2
    weight_one = 0.6 / (epsilon + smooth_one) ** 2
    weight_two = 0.3 / (epsilon + smooth_two) ** 2
    return (weight_zero * cand_zero + weight_one * cand_one + weight_two * cand_two) / (
        weight_zero + weight_one + weight_two
    )


def flux_along(extended, spatial_axis, alpha):
    direction = spatial_axis - 1
    density, velocity, pressure = primitives(extended)
    speed = velocity[direction]
    components = [
        extended[direction + 1],
        extended[1] * speed,
        extended[2] * speed,
        extended[3] * speed,
        (extended[4] + pressure) * speed,
    ]
    components[direction + 1] = components[direction + 1] + pressure
    fluxes = jnp.stack(components)
    right_going = 0.5 * (fluxes + alpha * extended)
    left_going = 0.5 * (fluxes - alpha * extended)
    length = extended.shape[spatial_axis] - 6

    def window(values, begin):
        return lax.slice_in_dim(values, begin, begin + length + 1, axis=spatial_axis)

    interface = reconstruct(
        window(right_going, 0),
        window(right_going, 1),
        window(right_going, 2),
        window(right_going, 3),
        window(right_going, 4),
    )
    interface = interface + reconstruct(
        window(left_going, 5),
        window(left_going, 4),
        window(left_going, 3),
        window(left_going, 2),
        window(left_going, 1),
    )
    return lax.slice_in_dim(interface, 0, length, axis=spatial_axis) - lax.slice_in_dim(
        interface, 1, length + 1, axis=spatial_axis
    )


def wrapped_depth(fields):
    return jnp.concatenate([fields[:, :, :, -3:], fields, fields[:, :, :, :3]], axis=3)


def evaluate(fields):
    alphas = lax.pmax(local_speeds(fields), ("gx", "gy"))
    padded = padded_2(fields, (("gx", 1), ("gy", 2)), 3)
    along_depth = flux_along(wrapped_depth(fields), 3, alphas[2])
    along_first = flux_along(padded[:, :, 3:-3, :], 1, alphas[0])
    along_second = flux_along(padded[:, 3:-3, :, :], 2, alphas[1])
    return along_first + along_second + along_depth


def local(initial, guesses):
    weights_table = jnp.array(radau_weights, jnp.float32)
    node_index = lax.axis_index("node")
    current = guesses[0]
    for sweep_index in range(SWEEPS):
        rate = evaluate(current)
        own_row = lax.dynamic_index_in_dim(weights_table, node_index, 0, keepdims=False)
        combined = jnp.sum(
            own_row[:, None, None, None, None]
            * lax.all_gather(rate[None], "node", axis=0, tiled=True),
            axis=0,
        )
        current = initial + step_size * combined
    return current[None]


def solution(mesh):
    placed = (P(None, "gx", "gy", None), P("node", None, "gx", "gy", None))
    return jax.shard_map(
        local,
        mesh=mesh,
        in_specs=placed,
        out_specs=P("node", None, "gx", "gy", None),
        check_vma=False,
    )
```

profile of v0, /device:TPU:1, one launch (start us, length us, event | category | flops | bytes accessed | tf_op | source)
XLA Modules:
  0.0 661.4 jit_solution(319501173477594485)
XLA Ops:
  6.5 1.0 fusion.69
  7.6 8.3 %collective-permute-start = (f32[5,3,16,128]{3,2,1,0:T(8,128)S(1)}, f32[5,3,16,128]{3,2,1,0:T(8,128)S(1)}, u32[]{:S(2)}, u32[]{:S(2)}) collective-permute-start(f32[5,3,16,128]{3,2,1,0:T(8,128)S(1)} %get-tuple-element.71), channel_id=1, source_target_pairs={{0,8},{8,16},{16,24},{24,32},{32,40},{40,48},{48,56},{56,64},{64,7... | collective-permute-start | bytes 368648 | tf_op jit(solution)/shard_map/ppermute | solution.py:29
  15.9 10.4 %collective-permute-start.1 = (f32[5,3,16,128]{3,2,1,0:T(8,128)S(1)}, f32[5,3,16,128]{3,2,1,0:T(8,128)S(1)}, u32[]{:S(2)}, u32[]{:S(2)}) collective-permute-start(f32[5,3,16,128]{3,2,1,0:T(8,128)S(1)} %get-tuple-element.72), channel_id=1, source_target_pairs={{8,0},{16,8},{24,16},{32,24},{40,32},{48,40},{56,48},{64,56},{72,6... | collective-permute-start | bytes 368648 | tf_op jit(solution)/shard_map/ppermute | solution.py:31
  29.0 247.8 %all-reduce.1 = (f32[]{:T(128)}, f32[]{:T(128)}, f32[]{:T(128)}) all-reduce(f32[]{:T(128)} %get-tuple-element.9, f32[]{:T(128)} %get-tuple-element.10, f32[]{:T(128)} %get-tuple-element.8), channel_id=1, replica_groups=mesh['node'=4,'gx'=16,'gy'=8] {'gx','gy'}, use_global_device_ids=true, to_apply=%region_9.0 | all-reduce | flops 3 | bytes 24 | tf_op jit(solution)/shard_map/pmax | solution.py:118
  276.8 0.9 add_multiply_fusion.1
  277.7 5.0 divide_add_fusion.1
  283.2 1.9 collective-permute-start.2
  285.1 5.0 collective-permute-start.3
  290.9 2.4 divide_add_fusion.5
  294.6 3.8 divide_add_fusion.3
  298.4 1.0 fusion.2
  300.2 31.4 %all-gather.5.cloned.1.call-done = f32[20,12,16,128]{3,2,1,0:T(8,128)} async-done(((f32[5,12,16,128]{3,2,1,0:T(8,128)}), f32[20,12,16,128]{3,2,1,0:T(8,128)}) %all-gather.5.cloned.1.call-update) | async-done | bytes 1966096 | tf_op jit(solution)/shard_map/all_gather | solution.py:135
  331.6 1.9 multiply_reduce_fusion.1
  333.8 7.1 %collective-permute-start.4 = (f32[5,3,16,128]{3,2,1,0:T(8,128)S(1)}, f32[5,3,16,128]{3,2,1,0:T(8,128)S(1)}, u32[]{:S(2)}, u32[]{:S(2)}) collective-permute-start(f32[5,3,16,128]{3,2,1,0:T(8,128)S(1)} %get-tuple-element.67), channel_id=1, source_target_pairs={{0,8},{8,16},{16,24},{24,32},{32,40},{40,48},{48,56},{56,64},{64,7... | collective-permute-start | bytes 368648 | tf_op jit(solution)/shard_map/ppermute | solution.py:29
  340.9 5.3 collective-permute-start.5
  347.9 248.0 %all-reduce = (f32[]{:T(128)}, f32[]{:T(128)}, f32[]{:T(128)}) all-reduce(f32[]{:T(128)} %get-tuple-element.6, f32[]{:T(128)} %get-tuple-element.7, f32[]{:T(128)} %get-tuple-element.5), channel_id=1, replica_groups=mesh['node'=4,'gx'=16,'gy'=8] {'gx','gy'}, use_global_device_ids=true, to_apply=%region_20.21 | all-reduce | flops 3 | bytes 24 | tf_op jit(solution)/shard_map/pmax | solution.py:118
  596.8 5.0 divide_add_fusion
  602.2 1.9 collective-permute-start.6
  604.1 5.4 collective-permute-start.7
  610.4 2.4 divide_add_fusion.4
  614.1 3.8 divide_add_fusion.2
  617.9 1.0 fusion
  618.9 33.0 %all-gather.7.cloned.1.call-done = f32[20,12,16,128]{3,2,1,0:T(8,128)} async-done(((f32[5,12,16,128]{3,2,1,0:T(8,128)}), f32[20,12,16,128]{3,2,1,0:T(8,128)}) %all-gather.7.cloned.1.call-update) | async-done | bytes 1966096 | tf_op jit(solution)/shard_map/all_gather | solution.py:135
  651.9 1.8 multiply_reduce_fusion
  (77 shorter events, 11.9 us)
Async XLA Ops:
  6.5 20.6 %copy-start = (f32[1,5,12,16,128]{4,3,2,1,0:T(8,128)S(1)}, f32[1,5,12,16,128]{4,3,2,1,0:T(8,128)}, u32[]{:S(2)}) copy-start(f32[1,5,12,16,128]{4,3,2,1,0:T(8,128)} %param.4) | copy-start | bytes 1474564
  6.5 325.1 %all-gather.5.cloned.1.call-start = ((), (), s32[]{:S(2)}) async-start(), calls=%async_computation | async-start | bytes 2457600 | tf_op jit(solution)/shard_map/all_gather | solution.py:135
  7.6 275.2 %collective-permute-start = (f32[5,3,16,128]{3,2,1,0:T(8,128)S(1)}, f32[5,3,16,128]{3,2,1,0:T(8,128)S(1)}, u32[]{:S(2)}, u32[]{:S(2)}) collective-permute-start(f32[5,3,16,128]{3,2,1,0:T(8,128)S(1)} %get-tuple-element.71), channel_id=1, source_target_pairs={{0,8},{8,16},{16,24},{24,32},{32,40},{40,48},{48,56},{56,64},{64,7... | collective-permute-start | bytes 368648 | tf_op jit(solution)/shard_map/ppermute | solution.py:29
  15.9 266.9 %collective-permute-start.1 = (f32[5,3,16,128]{3,2,1,0:T(8,128)S(1)}, f32[5,3,16,128]{3,2,1,0:T(8,128)S(1)}, u32[]{:S(2)}, u32[]{:S(2)}) collective-permute-start(f32[5,3,16,128]{3,2,1,0:T(8,128)S(1)} %get-tuple-element.72), channel_id=1, source_target_pairs={{8,0},{16,8},{24,16},{32,24},{40,32},{48,40},{56,48},{64,56},{72,6... | collective-permute-start | bytes 368648 | tf_op jit(solution)/shard_map/ppermute | solution.py:31
  283.2 10.2 %collective-permute-start.2 = (f32[5,18,3,128]{3,2,1,0:T(4,128)S(1)}, f32[5,18,3,128]{3,2,1,0:T(4,128)S(1)}, u32[]{:S(2)}, u32[]{:S(2)}) collective-permute-start(f32[5,18,3,128]{3,2,1,0:T(4,128)S(1)} %get-tuple-element.65), channel_id=1, source_target_pairs={{0,1},{1,2},{2,3},{3,4},{4,5},{5,6},{6,7},{7,0},{8,9},{9,10},{10,1... | collective-permute-start | bytes 414728 | tf_op jit(solution)/shard_map/ppermute | solution.py:29
  285.1 8.2 %collective-permute-start.3 = (f32[5,18,3,128]{3,2,1,0:T(4,128)S(1)}, f32[5,18,3,128]{3,2,1,0:T(4,128)S(1)}, u32[]{:S(2)}, u32[]{:S(2)}) collective-permute-start(f32[5,18,3,128]{3,2,1,0:T(4,128)S(1)} %get-tuple-element.66), channel_id=1, source_target_pairs={{1,0},{2,1},{3,2},{4,3},{5,4},{6,5},{7,6},{0,7},{9,8},{10,9},{11,1... | collective-permute-start | bytes 414728 | tf_op jit(solution)/shard_map/ppermute | solution.py:31
  299.4 352.5 %all-gather.7.cloned.1.call-start = ((), (), s32[]{:S(2)}) async-start(), calls=%async_computation.1 | async-start | bytes 2457600 | tf_op jit(solution)/shard_map/all_gather | solution.py:135
  331.6 1.9 copy-start.1
  333.8 268.0 %collective-permute-start.4 = (f32[5,3,16,128]{3,2,1,0:T(8,128)S(1)}, f32[5,3,16,128]{3,2,1,0:T(8,128)S(1)}, u32[]{:S(2)}, u32[]{:S(2)}) collective-permute-start(f32[5,3,16,128]{3,2,1,0:T(8,128)S(1)} %get-tuple-element.67), channel_id=1, source_target_pairs={{0,8},{8,16},{16,24},{24,32},{32,40},{40,48},{48,56},{56,64},{64,7... | collective-permute-start | bytes 368648 | tf_op jit(solution)/shard_map/ppermute | solution.py:29
  340.9 260.9 %collective-permute-start.5 = (f32[5,3,16,128]{3,2,1,0:T(8,128)S(1)}, f32[5,3,16,128]{3,2,1,0:T(8,128)S(1)}, u32[]{:S(2)}, u32[]{:S(2)}) collective-permute-start(f32[5,3,16,128]{3,2,1,0:T(8,128)S(1)} %get-tuple-element.68), channel_id=1, source_target_pairs={{8,0},{16,8},{24,16},{32,24},{40,32},{48,40},{56,48},{64,56},{72,6... | collective-permute-start | bytes 368648 | tf_op jit(solution)/shard_map/ppermute | solution.py:31
  602.2 10.6 %collective-permute-start.6 = (f32[5,18,3,128]{3,2,1,0:T(4,128)S(1)}, f32[5,18,3,128]{3,2,1,0:T(4,128)S(1)}, u32[]{:S(2)}, u32[]{:S(2)}) collective-permute-start(f32[5,18,3,128]{3,2,1,0:T(4,128)S(1)} %get-tuple-element.61), channel_id=1, source_target_pairs={{0,1},{1,2},{2,3},{3,4},{4,5},{5,6},{6,7},{7,0},{8,9},{9,10},{10,1... | collective-permute-start | bytes 414728 | tf_op jit(solution)/shard_map/ppermute | solution.py:29
  604.1 8.7 %collective-permute-start.7 = (f32[5,18,3,128]{3,2,1,0:T(4,128)S(1)}, f32[5,18,3,128]{3,2,1,0:T(4,128)S(1)}, u32[]{:S(2)}, u32[]{:S(2)}) collective-permute-start(f32[5,18,3,128]{3,2,1,0:T(4,128)S(1)} %get-tuple-element.62), channel_id=1, source_target_pairs={{1,0},{2,1},{3,2},{4,3},{5,4},{6,5},{7,6},{0,7},{9,8},{10,9},{11,1... | collective-permute-start | bytes 414728 | tf_op jit(solution)/shard_map/ppermute | solution.py:31
Sparse Core Ops, SparseCore 0:
  299.5 32.0 all-gather.4
  619.0 32.8 all-gather.6
where the time goes:
time: 662 us; the launch traced here: 661 us
  blocking collectives  496 us (75%)
  waiting for transfers between devices  64.5 us (10%)
  starting transfers between devices  45.4 us (7%)
  other arithmetic  39.6 us (6%)
  between operations  14 us (2%)
    pmax x2, blocking collectives, evaluate(): alphas = lax.pmax(local_speeds(fields), ('gx', 'gy'))  496 us
    all_gather x2, waiting for transfers between devices, local(): lax.all_gather(rate[None], 'node', axis=0, tiled=True)  64.4 us
    ppermute x4, starting transfers between devices, padded_2(): lax.ppermute(head, axis, [((i + 1) % count, i) for i in range(count)])  26.1 us
    add x6, other arithmetic, flux_along(): interface + reconstruct(window(left_going, 5), window(left_going, 4), win...  22.3 us
    ppermute x4, starting transfers between devices, padded_2(): lax.ppermute(tail, axis, [(i, (i + 1) % count) for i in range(count)])  19.2 us
  transfers between devices with their start and end apart: 10, of which 2 were waited for; matrix products, arithmetic and copies ran while one was open for 4% of the time, Pallas kernels for 0%

commit v1 on v0

v1 whole, which is shorter than its diff:
```python
import functools

import jax
import jax.numpy as jnp
from jax import lax
from jax.experimental import pallas as pl
from jax.experimental.pallas import tpu as pltpu
from jax.sharding import PartitionSpec as P

SWEEPS = 2
SCALE = 1.0 / 64.0

heat_ratio = 1.4
step_size = 0.025
density_floor = 0.5
pressure_floor = 0.25
epsilon = 1e-06
radau_weights = [
    [0.112999479323156, -0.040309220723522, 0.025802377420336, -0.009904676507266],
    [0.2343839957474, 0.206892573935359, -0.047857128048541, 0.016047422806516],
    [0.21668178462325, 0.406123263867373, 0.189036518170056, -0.024182104899833],
    [0.220462211176768, 0.388193468843172, 0.32884431998006, 0.0625],
]
MESH = pl.DeviceIdType.MESH
EPS = epsilon * 4.0 * SCALE * SCALE
NX, NY, LANES = 12, 16, 128
CHUNKS = ((3, 3), (6, 3), (0, 3), (9, 3))
YROWS = 40


def primitives(u):
    density = jnp.maximum(u[0], density_floor * SCALE)
    inverse = 1.0 / density
    velocity = [u[k] * inverse for k in (1, 2, 3)]
    kinetic = u[1] * velocity[0] + u[2] * velocity[1] + u[3] * velocity[2]
    pressure = jnp.maximum(0.4 * (u[4] - 0.5 * kinetic), pressure_floor * SCALE)
    return inverse, velocity, pressure


def flux(u, velocity, pressure, k):
    speed = velocity[k]
    parts = [u[k + 1], u[1] * speed, u[2] * speed, u[3] * speed, (u[4] + pressure) * speed]
    parts[k + 1] = parts[k + 1] + pressure
    return parts


class Line:
    def __init__(self, cells):
        self.cells = cells
        self.made = {}

    def get(self, name, i):
        key = (name, i)
        if key not in self.made:
            self.made[key] = getattr(self, "make_" + name)(i)
        return self.made[key]

    def g(self, i):
        return self.cells[i]

    def make_d(self, i):
        return self.cells[i + 1] - self.cells[i]

    def make_e(self, i):
        return self.get("d", i + 1) - self.get("d", i)

    def make_t(self, i):
        return self.get("e", i + 1) - self.get("e", i)

    def make_p(self, i):
        d = self.get("d", i)
        return d * d + EPS

    def make_k(self, i):
        e = self.get("e", i)
        return (4.0 / 3.0) * (e * e)

    def make_x(self, i):
        return self.get("e", i) * self.get("d", i)

    def make_q(self, i):
        return self.get("k", i) + self.get("p", i)

    def make_l(self, i):
        s = self.get("k", i) + self.get("e", i) * self.get("d", i + 1) + self.get("p", i + 1)
        return s * s

    def make_m(self, i):
        s = self.get("q", i) + self.get("x", i)
        return s * s

    def make_r(self, i):
        s = self.get("q", i) - self.get("x", i)
        return s * s


def correction(s0, s1, s2, t0, t2):
    a = 3.0 * s0
    r2 = s2 + s2
    total = s1 * s2 + a * (r2 + s1)
    return (s1 * (1.0 / total)) * (r2 * t0 + a * t2)


def interface(plus, minus, i):
    cp = correction(
        plus.get("l", i - 2), plus.get("m", i - 1), plus.get("r", i),
        plus.get("t", i - 2), plus.get("t", i - 1),
    )
    cm = correction(
        minus.get("r", i + 1), minus.get("m", i), minus.get("l", i - 1),
        minus.get("t", i), minus.get("t", i - 1),
    )
    near = plus.get("d", i) - minus.get("d", i)
    far = plus.get("d", i - 1) - minus.get("d", i + 1)
    return (plus.g(i) + minus.g(i + 1)) + (1.0 / 6.0) * ((near + near) + far + (cm - cp))


def pick(index, values):
    out = jnp.float32(values[-1])
    for k in range(len(values) - 2, -1, -1):
        out = jnp.where(index == k, jnp.float32(values[k]), out)
    return out


def kernel(
    sizes, init_hbm, guess_hbm, out_hbm,
    w, fx, fy, fz, gs, hs, hx, rate, r1, s2, r2, init, stage,
    ysend, yrecv, fyp, part, amsg, ar1, amid, ar2, alpha,
    load_sem, out_sem, xs_sem, xr_sem, ys_sem, yr_sem,
    a1s_sem, a1r_sem, a2s_sem, a2r_sem, e1s_sem, e1r_sem, e2s_sem, e2r_sem,
):
    n_gx, n_gy = sizes
    n_z, n_y = n_gx // 2, 2 * n_gy
    node, gx, gy = lax.axis_index("node"), lax.axis_index("gx"), lax.axis_index("gy")
    mate_a = node + 1 - 2 * lax.rem(node, 2)
    mate_b = 3 - node
    z, hi = gx // 2, lax.rem(gx, 2)
    y = hi * n_gy + gy

    def y_peer(step):
        other = lax.rem(y + step, n_y)
        return {"gx": z * 2 + other // n_gy, "gy": lax.rem(other, n_gy)}

    def z_peer(step):
        return {"gx": lax.rem(z + step, n_z) * 2 + hi}

    up_x = {"gx": lax.rem(gx + 1, n_gx)}
    down_x = {"gx": lax.rem(gx + n_gx - 1, n_gx)}
    up_y = {"gy": lax.rem(gy + 1, n_gy)}
    down_y = {"gy": lax.rem(gy + n_gy - 1, n_gy)}
    first_mates = ({"node": mate_a}, {"node": mate_b})
    second_mates = ({"node": mate_b}, {"node": mate_a})

    load_init = pltpu.make_async_copy(init_hbm, init, load_sem.at[0])
    load_guess = pltpu.make_async_copy(guess_hbm.at[0], stage, load_sem.at[1])
    load_guess.start()
    load_init.start()

    barrier = pltpu.get_barrier_semaphore()
    greeted = [y_peer(k) for k in range(1, n_y)] + [z_peer(k) for k in range(1, n_z)]
    greeted += [up_x, down_x, {"node": mate_a}, {"node": mate_b}]
    for peer in greeted:
        pl.semaphore_signal(barrier, inc=1, device_id=peer, device_id_type=MESH)

    def entry(f):
        return pick(node, [0.5 * step_size * f(m, m + 1 - 2 * (m % 2), 3 - m) for m in range(4)])

    table = radau_weights
    own = entry(lambda m, a, b: table[m][m])
    got = (entry(lambda m, a, b: table[m][a]), entry(lambda m, a, b: table[m][b]))
    give_own = (entry(lambda m, a, b: table[b][m]), entry(lambda m, a, b: table[a][m]))
    give_got = (entry(lambda m, a, b: table[b][a]), entry(lambda m, a, b: table[a][b]))

    def rows(h):
        return slice(8 + 8 * h, 16 + 8 * h)

    def half(h):
        return slice(8 * h, 8 * h + 8)

    def take_plane(s, p, fields):
        best = [part[k] for k in range(3)]
        for h in range(2):
            u = fields[h]
            inverse, velocity, pressure = primitives(u)
            sound = jnp.sqrt(heat_ratio * pressure * inverse)
            for k in range(3):
                best[k] = jnp.maximum(best[k], jnp.abs(velocity[k]) + sound)
            f0, f1, f2 = (flux(u, velocity, pressure, k) for k in range(3))
            for c in range(5):
                w[s, c, p + 3, rows(h), :] = u[c]
                fx[c, p + 3, half(h), :] = f0[c]
                fy[c, p, rows(h), :] = f1[c]
                fz[c, p, half(h), :] = f2[c]
        for k in range(3):
            part[k] = best[k]

    for k in range(3):
        part[k] = jnp.zeros((8, LANES), jnp.float32)
    load_guess.wait()

    def first(p, _):
        take_plane(0, p, [[stage[c, p, half(h), :] * SCALE for c in range(5)] for h in range(2)])
        return 0

    lax.fori_loop(0, NX, first, 0)
    load_init.wait()
    pl.semaphore_wait(barrier, len(greeted))

    def x_halo(s):
        low = pltpu.make_async_remote_copy(
            src_ref=w.at[s, :, pl.ds(3, 3), pl.ds(8, 16), :], dst_ref=w.at[s, :, pl.ds(15, 3), pl.ds(8, 16), :],
            send_sem=xs_sem.at[0], recv_sem=xr_sem.at[s, 0], device_id=down_x, device_id_type=MESH)
        high = pltpu.make_async_remote_copy(
            src_ref=w.at[s, :, pl.ds(12, 3), pl.ds(8, 16), :], dst_ref=w.at[s, :, pl.ds(0, 3), pl.ds(8, 16), :],
            send_sem=xs_sem.at[1], recv_sem=xr_sem.at[s, 1], device_id=up_x, device_id_type=MESH)
        return low, high

    def y_halo(s):
        low = pltpu.make_async_remote_copy(
            src_ref=ysend.at[0], dst_ref=yrecv.at[s, 1],
            send_sem=ys_sem.at[0], recv_sem=yr_sem.at[s, 1], device_id=down_y, device_id_type=MESH)
        high = pltpu.make_async_remote_copy(
            src_ref=ysend.at[1], dst_ref=yrecv.at[s, 0],
            send_sem=ys_sem.at[1], recv_sem=yr_sem.at[s, 0], device_id=up_y, device_id_type=MESH)
        return low, high

    def swap(s, h, chunk, second):
        start, count = CHUNKS[chunk]
        span = pl.ds(start, count)
        return pltpu.make_async_remote_copy(
            src_ref=(s2 if second else rate).at[h, span], dst_ref=(r2 if second else r1).at[s, h, span],
            send_sem=(e2s_sem if second else e1s_sem).at[h, chunk],
            recv_sem=(e2r_sem if second else e1r_sem).at[s, h, chunk],
            device_id=(second_mates if second else first_mates)[h], device_id_type=MESH)

    def x_pass(s, cells, faces, planes, saved_in, saved_out):
        def body(c, _):
            a = alpha[0]
            for h in range(2):
                up, down = {}, {}
                for i in cells:
                    f = fx[c, i, half(h), :]
                    au = a * w[s, c, i, rows(h), :]
                    up[i] = f + au
                    down[i] = f - au
                up, down = Line(up), Line(down)
                flows = {}
                for i, slot in saved_in:
                    flows[i] = hx[slot, h, c]
                for i in faces:
                    flows[i] = interface(up, down, i - 1)
                for i, slot in saved_out:
                    hx[slot, h, c] = flows[i]
                for i in planes:
                    rate[h, i - 3, c] = flows[i] - flows[i + 1]
            return 0

        lax.fori_loop(0, 5, body, 0)

    def yz_plane(s, p):
        a1 = alpha[1]
        a2 = alpha[2]
        for c in range(5):
            for j in range(4):
                tile = slice(8 * j, 8 * j + 8)
                f = fy[c, p, tile, :]
                au = a1 * w[s, c, p + 3, tile, :]
                gs[0, c, tile, :] = f + au
                gs[1, c, tile, :] = f - au
        for c in range(5):
            for j in range(3):
                base = 8 + 8 * j
                up = Line({i: gs[0, c, base - 1 + i : base + 7 + i, :] for i in range(-2, 3)})
                down = Line({i: gs[1, c, base - 1 + i : base + 7 + i, :] for i in range(-1, 4)})
                hs[c, 8 * j : 8 * j + 8, :] = interface(up, down, 0)
        for c in range(5):
            for h in range(2):
                f = fz[c, p, half(h), :]
                au = a2 * w[s, c, p + 3, rows(h), :]
                right, left = f + au, f - au
                up = Line({i: right if i == 0 else pltpu.roll(right, (-i) % LANES, 1) for i in range(-2, 3)})
                down = Line({i: left if i == 0 else pltpu.roll(left, (-i) % LANES, 1) for i in range(-1, 4)})
                flow = interface(up, down, 0)
                along_z = pltpu.roll(flow, 1, 1) - flow
                along_y = hs[c, half(h), :] - hs[c, 8 * h + 1 : 8 * h + 9, :]
                rate[h, p, c] = rate[h, p, c] + (along_y + along_z)

    def combine(s, chunk):
        start, count = CHUNKS[chunk]
        for h in range(2):
            swap(s, h, chunk, False).wait_recv()

            def body(p, _, h=h):
                for c in range(5):
                    s2[h, p, c] = give_own[h] * rate[h, p, c] + give_got[h] * r1[s, h, p, c]
                return 0

            lax.fori_loop(start, start + count, body, 0)
            swap(s, h, chunk, True).start()

    def finish(s, chunk):
        start, count = CHUNKS[chunk]
        for h in range(2):
            swap(s, h, chunk, True).wait_recv()

        def updated(p):
            return [
                [
                    init[c, p, half(h), :] * SCALE
                    + (own * rate[h, p, c] + (got[h] * r1[s, h, p, c] + r2[s, h, p, c]))
                    for c in range(5)
                ]
                for h in range(2)
            ]

        @pl.when(s < SWEEPS - 1)
        def _():
            def body(p, _):
                take_plane(s + 1, p, updated(p))
                return 0

            lax.fori_loop(start, start + count, body, 0)

        @pl.when(s == SWEEPS - 1)
        def _():
            def body(p, _):
                fields = updated(p)
                for h in range(2):
                    for c in range(5):
                        stage[c, p, half(h), :] = fields[h][c] * (1.0 / SCALE)
                return 0

            lax.fori_loop(start, start + count, body, 0)

    def whole(ref, sem):
        return pltpu.make_async_copy(ref, ref, sem)

    def sweep(s, _):
        for k in range(3):
            amsg[k : k + 1, :] = jnp.max(part[k], axis=0, keepdims=True)
        for k in range(1, n_y):
            pltpu.make_async_remote_copy(
                src_ref=amsg, dst_ref=ar1.at[s, k - 1], send_sem=a1s_sem, recv_sem=a1r_sem.at[s],
                device_id=y_peer(k), device_id_type=MESH).start()
        for copy in x_halo(s):
            copy.start()
        for c in range(5):
            for p in range(NX):
                ysend[0, c, 3 * p : 3 * p + 3, :] = w[s, c, p + 3, 8:11, :]
                ysend[1, c, 3 * p : 3 * p + 3, :] = w[s, c, p + 3, 21:24, :]
        for copy in y_halo(s):
            copy.start()
        whole(ar1.at[s], a1r_sem.at[s]).wait()
        best = amsg[...]
        for k in range(n_y - 1):
            best = jnp.maximum(best, ar1[s, k])
        amid[...] = best
        for k in range(1, n_z):
            pltpu.make_async_remote_copy(
                src_ref=amid, dst_ref=ar2.at[s, k - 1], send_sem=a2s_sem, recv_sem=a2r_sem.at[s],
                device_id=z_peer(k), device_id_type=MESH).start()

        for side, copy in ((1, y_halo(s)[0]), (0, y_halo(s)[1])):
            copy.wait_recv()
            for j in range(5):
                tile = slice(8 * j, 8 * j + 8)
                u = [yrecv[s, side, c, tile, :] for c in range(5)]
                _, velocity, pressure = primitives(u)
                parts = flux(u, velocity, pressure, 1)
                for c in range(5):
                    fyp[side, c, tile, :] = parts[c]
            at = slice(5, 8) if side == 0 else slice(24, 27)
            for c in range(5):
                for p in range(NX):
                    w[s, c, p + 3, at, :] = yrecv[s, side, c, 3 * p : 3 * p + 3, :]
                    fy[c, p, at, :] = fyp[side, c, 3 * p : 3 * p + 3, :]

        if n_z > 1:
            whole(ar2.at[s], a2r_sem.at[s]).wait()
            best = amid[...]
            for k in range(n_z - 1):
                best = jnp.maximum(best, ar2[s, k])
        for k in range(3):
            top = jnp.max(best[k : k + 1, :], axis=1, keepdims=True)
            alpha[k] = jnp.broadcast_to(top, (8, LANES))
            part[k] = jnp.zeros((8, LANES), jnp.float32)

        x_pass(s, range(3, 15), range(6, 13), range(6, 12), (), ((6, 0), (12, 1)))

        def run(chunk):
            start, count = CHUNKS[chunk]

            def body(p, _):
                yz_plane(s, p)
                return 0

            lax.fori_loop(start, start + count, body, 0)
            for h in range(2):
                swap(s, h, chunk, False).start()

        run(0)
        run(1)
        low, high = x_halo(s)
        low.wait_recv()
        high.wait_recv()

        def halo_plane(i, _):
            i = jnp.where(i < 3, i, i + 12)
            for h in range(2):
                u = [w[s, c, i, rows(h), :] for c in range(5)]
                _, velocity, pressure = primitives(u)
                parts = flux(u, velocity, pressure, 0)
                for c in range(5):
                    fx[c, i, half(h), :] = parts[c]
            return 0

        lax.fori_loop(0, 6, halo_plane, 0)
        x_pass(s, range(0, 8), range(3, 6), range(3, 6), ((6, 0),), ())
        x_pass(s, range(10, 18), range(13, 16), range(12, 15), ((12, 1),), ())
        combine(s, 0)
        run(2)
        combine(s, 1)
        run(3)
        low.wait_send()
        high.wait_send()
        for copy in y_halo(s):
            copy.wait_send()
        whole(ar1.at[s], a1s_sem).wait()
        if n_z > 1:
            whole(ar2.at[s], a2s_sem).wait()
        finish(s, 0)
        combine(s, 2)
        finish(s, 1)
        combine(s, 3)
        finish(s, 2)
        finish(s, 3)
        for chunk in range(len(CHUNKS)):
            for h in range(2):
                swap(s, h, chunk, False).wait_send()
                swap(s, h, chunk, True).wait_send()
        return 0

    lax.fori_loop(0, SWEEPS, sweep, 0)
    store = pltpu.make_async_copy(stage, out_hbm.at[0], out_sem)
    store.start()
    store.wait()


def call(sizes, initial, guesses):
    n_z, n_y = sizes[0] // 2, 2 * sizes[1]
    f32 = jnp.float32
    dma = pltpu.SemaphoreType.DMA
    chunks = len(CHUNKS)
    tile = (8, LANES)

    def vm(*shape):
        return pltpu.VMEM(shape, f32)

    return pl.pallas_call(
        functools.partial(kernel, sizes),
        out_shape=jax.ShapeDtypeStruct(guesses.shape, f32),
        in_specs=[pl.BlockSpec(memory_space=pl.ANY)] * 2,
        out_specs=pl.BlockSpec(memory_space=pl.ANY),
        scratch_shapes=[
            vm(SWEEPS, 5, NX + 6, 32, LANES),
            vm(5, NX + 6, NY, LANES),
            vm(5, NX, 32, LANES),
            vm(5, NX, NY, LANES),
            vm(2, 5, 40, LANES),
            vm(5, 24, LANES),
            vm(2, 2, 5, *tile),
            vm(2, NX, 5, *tile),
            vm(SWEEPS, 2, NX, 5, *tile),
            vm(2, NX, 5, *tile),
            vm(SWEEPS, 2, NX, 5, *tile),
            vm(5, NX, NY, LANES),
            vm(5, NX, NY, LANES),
            vm(2, 5, YROWS, LANES),
            vm(SWEEPS, 2, 5, YROWS, LANES),
            vm(2, 5, YROWS, LANES),
            vm(3, *tile),
            vm(*tile),
            vm(SWEEPS, n_y - 1, *tile),
            vm(*tile),
            vm(SWEEPS, max(n_z - 1, 1), *tile),
            vm(3, *tile),
            dma((2,)), dma,
            dma((2,)), dma((SWEEPS, 2)), dma((2,)), dma((SWEEPS, 2)),
            dma, dma((SWEEPS,)), dma, dma((SWEEPS,)),
            dma((2, chunks)), dma((SWEEPS, 2, chunks)), dma((2, chunks)), dma((SWEEPS, 2, chunks)),
        ],
        compiler_params=pltpu.CompilerParams(
            collective_id=0, has_side_effects=True, vmem_limit_bytes=40 << 20
        ),
    )(initial, guesses)


def solution(mesh):
    sizes = (mesh.shape["gx"], mesh.shape["gy"])
    placed = (P(None, "gx", "gy", None), P("node", None, "gx", "gy", None))
    return jax.shard_map(
        functools.partial(call, sizes),
        mesh=mesh,
        in_specs=placed,
        out_specs=P("node", None, "gx", "gy", None),
        check_vma=False,
    )
```

time: 662 us -> 87.8 us (0.13)
  the two profiles are of different devices: /device:TPU:1 before, /device:TPU:10 now
where the time goes in v1:
time: 87.8 us; the launch traced here: 87.6 us
  Pallas kernels  84.8 us (97%)
  local copies, waits for them, and re-layouts  2.84 us (3%)
    pallas_call x1, Pallas kernels, call(): pl.pallas_call(functools.partial(kernel, sizes), out_shape=jax.ShapeDtype...  84.8 us
    unnamed x5, local copies, waits for them, and re-layouts  2.84 us

profile of v1, /device:TPU:10, one launch (start us, length us, event | category | flops | bytes accessed | tf_op | source)
XLA Modules:
  0.0 87.6 jit_solution(6315200733116628378)
XLA Ops:
  0.0 0.0 copy-start
  0.0 1.0 %copy-done = f32[5,12,16,128]{3,2,1,0:T(8,128)S(1)} copy-done((f32[5,12,16,128]{3,2,1,0:T(8,128)S(1)}, f32[5,12,16,128]{3,2,1,0:T(8,128)}, u32[]{:S(2)}) %copy-start) | copy-done | bytes 491544
  1.0 0.0 copy-start.1
  1.0 1.0 %copy-done.1 = f32[1,5,12,16,128]{4,3,2,1,0:T(8,128)S(1)} copy-done((f32[1,5,12,16,128]{4,3,2,1,0:T(8,128)S(1)}, f32[1,5,12,16,128]{4,3,2,1,0:T(8,128)}, u32[]{:S(2)}) %copy-start.1) | copy-done | bytes 491544
  2.1 84.8 %shard_map.28 = f32[1,5,12,16,128]{4,3,2,1,0:T(8,128)S(1)} custom-call(f32[5,12,16,128]{3,2,1,0:T(8,128)S(1)} %copy-done, f32[1,5,12,16,128]{4,3,2,1,0:T(8,128)S(1)} %copy-done.1), custom_call_target="tpu_custom_call" | custom-call | tf_op jit(solution)/shard_map/pallas_call | solution.py:459
  86.9 0.8 copy.4
Async XLA Ops:
  0.0 1.0 %copy-start = (f32[5,12,16,128]{3,2,1,0:T(8,128)S(1)}, f32[5,12,16,128]{3,2,1,0:T(8,128)}, u32[]{:S(2)}) copy-start(f32[5,12,16,128]{3,2,1,0:T(8,128)} %init_hbm.1) | copy-start | bytes 1474564
  1.0 1.0 %copy-start.1 = (f32[1,5,12,16,128]{4,3,2,1,0:T(8,128)S(1)}, f32[1,5,12,16,128]{4,3,2,1,0:T(8,128)}, u32[]{:S(2)}) copy-start(f32[1,5,12,16,128]{4,3,2,1,0:T(8,128)} %guess_hbm.1) | copy-start | bytes 1474564

commit v2 on v1

--- a/solution.py
+++ b/solution.py
@@ -171,6 +171,8 @@
     give_own = (entry(lambda m, a, b: table[b][m]), entry(lambda m, a, b: table[a][m]))
     give_got = (entry(lambda m, a, b: table[b][a]), entry(lambda m, a, b: table[a][b]))
 
+    lane = lax.broadcasted_iota(jnp.int32, (1, LANES), 1)
+
     def rows(h):
         return slice(8 + 8 * h, 16 + 8 * h)
 
@@ -233,7 +235,7 @@
             recv_sem=(e2r_sem if second else e1r_sem).at[s, h, chunk],
             device_id=(second_mates if second else first_mates)[h], device_id_type=MESH)
 
-    def x_pass(s, cells, faces, planes, saved_in, saved_out):
+    def x_pass(s, cells, faces, planes, saved_in, saved_out, add):
         def body(c, _):
             a = alpha[0]
             for h in range(2):
@@ -252,12 +254,13 @@
                 for i, slot in saved_out:
                     hx[slot, h, c] = flows[i]
                 for i in planes:
-                    rate[h, i - 3, c] = flows[i] - flows[i + 1]
+                    along_x = flows[i] - flows[i + 1]
+                    rate[h, i - 3, c] = rate[h, i - 3, c] + along_x if add else along_x
             return 0
 
         lax.fori_loop(0, 5, body, 0)
 
-    def yz_plane(s, p):
+    def yz_plane(s, p, add):
         a1 = alpha[1]
         a2 = alpha[2]
         for c in range(5):
@@ -283,7 +286,8 @@
                 flow = interface(up, down, 0)
                 along_z = pltpu.roll(flow, 1, 1) - flow
                 along_y = hs[c, half(h), :] - hs[c, 8 * h + 1 : 8 * h + 9, :]
-                rate[h, p, c] = rate[h, p, c] + (along_y + along_z)
+                along = along_y + along_z
+                rate[h, p, c] = rate[h, p, c] + along if add else along
 
     def combine(s, chunk):
         start, count = CHUNKS[chunk]
@@ -336,14 +340,12 @@
         return pltpu.make_async_copy(ref, ref, sem)
 
     def sweep(s, _):
-        for k in range(3):
-            amsg[k : k + 1, :] = jnp.max(part[k], axis=0, keepdims=True)
+        tops = [jnp.max(part[k], axis=(0, 1), keepdims=True) for k in range(3)]
+        amsg[...] = jnp.where(lane < 43, tops[0], jnp.where(lane < 86, tops[1], tops[2]))
         for k in range(1, n_y):
             pltpu.make_async_remote_copy(
                 src_ref=amsg, dst_ref=ar1.at[s, k - 1], send_sem=a1s_sem, recv_sem=a1r_sem.at[s],
                 device_id=y_peer(k), device_id_type=MESH).start()
-        for copy in x_halo(s):
-            copy.start()
         for c in range(5):
             for p in range(NX):
                 ysend[0, c, 3 * p : 3 * p + 3, :] = w[s, c, p + 3, 8:11, :]
@@ -351,6 +353,8 @@
         for copy in y_halo(s):
             copy.start()
         whole(ar1.at[s], a1r_sem.at[s]).wait()
+        for copy in x_halo(s):
+            copy.start()
         best = amsg[...]
         for k in range(n_y - 1):
             best = jnp.maximum(best, ar1[s, k])
@@ -380,60 +384,68 @@
             best = amid[...]
             for k in range(n_z - 1):
                 best = jnp.maximum(best, ar2[s, k])
+        bounds = (0, 43, 86, LANES)
         for k in range(3):
-            top = jnp.max(best[k : k + 1, :], axis=1, keepdims=True)
-            alpha[k] = jnp.broadcast_to(top, (8, LANES))
+            mine = jnp.where((lane >= bounds[k]) & (lane < bounds[k + 1]), best, 0.0)
+            alpha[k] = jnp.broadcast_to(jnp.max(mine, axis=1, keepdims=True), (8, LANES))
             part[k] = jnp.zeros((8, LANES), jnp.float32)
 
-        x_pass(s, range(3, 15), range(6, 13), range(6, 12), (), ((6, 0), (12, 1)))
-
-        def run(chunk):
+        def run(chunk, add):
             start, count = CHUNKS[chunk]
 
             def body(p, _):
-                yz_plane(s, p)
+                yz_plane(s, p, add)
                 return 0
 
             lax.fori_loop(start, start + count, body, 0)
+
+        def send(chunk):
             for h in range(2):
                 swap(s, h, chunk, False).start()
 
-        run(0)
-        run(1)
-        low, high = x_halo(s)
-        low.wait_recv()
-        high.wait_recv()
-
-        def halo_plane(i, _):
-            i = jnp.where(i < 3, i, i + 12)
-            for h in range(2):
-                u = [w[s, c, i, rows(h), :] for c in range(5)]
-                _, velocity, pressure = primitives(u)
-                parts = flux(u, velocity, pressure, 0)
-                for c in range(5):
-                    fx[c, i, half(h), :] = parts[c]
-            return 0
-
-        lax.fori_loop(0, 6, halo_plane, 0)
-        x_pass(s, range(0, 8), range(3, 6), range(3, 6), ((6, 0),), ())
-        x_pass(s, range(10, 18), range(13, 16), range(12, 15), ((12, 1),), ())
+        def halo_planes(first):
+            def body(i, _):
+                for h in range(2):
+                    u = [w[s, c, i, rows(h), :] for c in range(5)]
+                    _, velocity, pressure = primitives(u)
+                    parts = flux(u, velocity, pressure, 0)
+                    for c in range(5):
+                        fx[c, i, half(h), :] = parts[c]
+                return 0
+
+            lax.fori_loop(first, first + 3, body, 0)
+
+        to_low, to_high = x_halo(s)
+        x_pass(s, range(3, 15), range(6, 13), range(6, 12), (), ((6, 0), (12, 1)), False)
+        run(0, True)
+        send(0)
+        run(1, True)
+        send(1)
+        run(2, False)
         combine(s, 0)
-        run(2)
+        to_low.wait_recv()
+        halo_planes(15)
+        x_pass(s, range(10, 18), range(13, 16), range(12, 15), ((12, 1),), (), False)
+        run(3, True)
+        send(3)
         combine(s, 1)
-        run(3)
-        low.wait_send()
-        high.wait_send()
+        to_high.wait_recv()
+        halo_planes(0)
+        x_pass(s, range(0, 8), range(3, 6), range(3, 6), ((6, 0),), (), True)
+        send(2)
+        to_low.wait_send()
+        to_high.wait_send()
         for copy in y_halo(s):
             copy.wait_send()
         whole(ar1.at[s], a1s_sem).wait()
         if n_z > 1:
             whole(ar2.at[s], a2s_sem).wait()
         finish(s, 0)
+        combine(s, 3)
+        finish(s, 1)
         combine(s, 2)
-        finish(s, 1)
-        combine(s, 3)
+        finish(s, 3)
         finish(s, 2)
-        finish(s, 3)
         for chunk in range(len(CHUNKS)):
             for h in range(2):
                 swap(s, h, chunk, False).wait_send()
@@ -479,10 +491,10 @@
             vm(SWEEPS, 2, 5, YROWS, LANES),
             vm(2, 5, YROWS, LANES),
             vm(3, *tile),
-            vm(*tile),
-            vm(SWEEPS, n_y - 1, *tile),
-            vm(*tile),
-            vm(SWEEPS, max(n_z - 1, 1), *tile),
+            vm(1, LANES),
+            vm(SWEEPS, n_y - 1, 1, LANES),
+            vm(1, LANES),
+            vm(SWEEPS, max(n_z - 1, 1), 1, LANES),
             vm(3, *tile),
             dma((2,)), dma,
             dma((2,)), dma((SWEEPS, 2)), dma((2,)), dma((SWEEPS, 2)),
@@ -490,7 +502,7 @@
             dma((2, chunks)), dma((SWEEPS, 2, chunks)), dma((2, chunks)), dma((SWEEPS, 2, chunks)),
         ],
         compiler_params=pltpu.CompilerParams(
-            collective_id=0, has_side_effects=True, vmem_limit_bytes=40 << 20
+            collective_id=0, has_side_effects=True, vmem_limit_bytes=60 << 20
         ),
     )(initial, guesses)
 

time: 87.8 us -> 73.9 us (0.84)
  the two profiles are of different devices: /device:TPU:10 before, /device:TPU:8 now
where the time goes in v2:
time: 73.9 us; the launch traced here: 73.8 us
  Pallas kernels  71.9 us (97%)
  local copies, waits for them, and re-layouts  1.85 us (3%)
    pallas_call x1, Pallas kernels, call(): pl.pallas_call(functools.partial(kernel, sizes), out_shape=jax.ShapeDtype...  71.9 us
    unnamed x1, local copies, waits for them, and re-layouts  1.85 us

profile of v2, /device:TPU:8, one launch (start us, length us, event | category | flops | bytes accessed | tf_op | source)
XLA Modules:
  0.0 73.8 jit_solution(9209425618314722978)
XLA Ops:
  0.0 71.9 %shard_map.28 = f32[1,5,12,16,128]{4,3,2,1,0:T(8,128)} custom-call(f32[5,12,16,128]{3,2,1,0:T(8,128)} %init_hbm.1, f32[1,5,12,16,128]{4,3,2,1,0:T(8,128)} %guess_hbm.1), custom_call_target="tpu_custom_call" | custom-call | tf_op jit(solution)/shard_map/pallas_call | solution.py:471
  71.9 1.9 %copy.4 = f32[1,5,12,16,128]{4,3,2,1,0:T(8,128)} copy(f32[1,5,12,16,128]{4,3,2,1,0:T(8,128)} %shard_map.28) | data formatting | bytes 983040

commit v3 on v2

--- a/solution.py
+++ b/solution.py
@@ -24,7 +24,7 @@
 MESH = pl.DeviceIdType.MESH
 EPS = epsilon * 4.0 * SCALE * SCALE
 NX, NY, LANES = 12, 16, 128
-CHUNKS = ((3, 3), (6, 3), (0, 3), (9, 3))
+CHUNKS = ((3, 2), (5, 2), (7, 2), (9, 3), (0, 2), (2, 1))
 YROWS = 40
 
 
@@ -268,14 +268,17 @@
                 tile = slice(8 * j, 8 * j + 8)
                 f = fy[c, p, tile, :]
                 au = a1 * w[s, c, p + 3, tile, :]
-                gs[0, c, tile, :] = f + au
-                gs[1, c, tile, :] = f - au
+                gs[0, slice(40 * c + 8 * j, 40 * c + 8 * j + 8), :] = f + au
+                gs[1, slice(40 * c + 8 * j, 40 * c + 8 * j + 8), :] = f - au
         for c in range(5):
-            for j in range(3):
-                base = 8 + 8 * j
-                up = Line({i: gs[0, c, base - 1 + i : base + 7 + i, :] for i in range(-2, 3)})
-                down = Line({i: gs[1, c, base - 1 + i : base + 7 + i, :] for i in range(-1, 4)})
-                hs[c, 8 * j : 8 * j + 8, :] = interface(up, down, 0)
+            for j in range(2):
+                base = 40 * c + 8 + 8 * j
+                up = Line({i: gs[0, base - 1 + i : base + 7 + i, :] for i in range(-2, 3)})
+                down = Line({i: gs[1, base - 1 + i : base + 7 + i, :] for i in range(-1, 4)})
+                hs[24 * c + 8 * j : 24 * c + 8 * j + 8, :] = interface(up, down, 0)
+        up = Line({i: gs[0, pl.ds(23 + i, 8, stride=40), :] for i in range(-2, 3)})
+        down = Line({i: gs[1, pl.ds(23 + i, 8, stride=40), :] for i in range(-1, 4)})
+        hs[pl.ds(16, 8, stride=24), :] = interface(up, down, 0)
         for c in range(5):
             for h in range(2):
                 f = fz[c, p, half(h), :]
@@ -285,7 +288,8 @@
                 down = Line({i: left if i == 0 else pltpu.roll(left, (-i) % LANES, 1) for i in range(-1, 4)})
                 flow = interface(up, down, 0)
                 along_z = pltpu.roll(flow, 1, 1) - flow
-                along_y = hs[c, half(h), :] - hs[c, 8 * h + 1 : 8 * h + 9, :]
+                row = 24 * c + 8 * h
+                along_y = hs[row : row + 8, :] - hs[row + 1 : row + 9, :]
                 along = along_y + along_z
                 rate[h, p, c] = rate[h, p, c] + along if add else along
 
@@ -331,10 +335,15 @@
                 fields = updated(p)
                 for h in range(2):
                     for c in range(5):
-                        stage[c, p, half(h), :] = fields[h][c] * (1.0 / SCALE)
+                        stage[c, p, half(h), :] = fields[h][c]
                 return 0
 
             lax.fori_loop(start, start + count, body, 0)
+            store(chunk).start()
+
+    def store(chunk):
+        span = pl.ds(*CHUNKS[chunk])
+        return pltpu.make_async_copy(stage.at[:, span], out_hbm.at[0, :, span], out_sem.at[chunk])
 
     def whole(ref, sem):
         return pltpu.make_async_copy(ref, ref, sem)
@@ -390,9 +399,7 @@
             alpha[k] = jnp.broadcast_to(jnp.max(mine, axis=1, keepdims=True), (8, LANES))
             part[k] = jnp.zeros((8, LANES), jnp.float32)
 
-        def run(chunk, add):
-            start, count = CHUNKS[chunk]
-
+        def run(start, count, add):
             def body(p, _):
                 yz_plane(s, p, add)
                 return 0
@@ -417,22 +424,23 @@
 
         to_low, to_high = x_halo(s)
         x_pass(s, range(3, 15), range(6, 13), range(6, 12), (), ((6, 0), (12, 1)), False)
-        run(0, True)
-        send(0)
-        run(1, True)
-        send(1)
-        run(2, False)
+        for chunk in range(3):
+            run(*CHUNKS[chunk], True)
+            send(chunk)
         combine(s, 0)
+        run(0, 3, False)
+        combine(s, 1)
         to_low.wait_recv()
         halo_planes(15)
         x_pass(s, range(10, 18), range(13, 16), range(12, 15), ((12, 1),), (), False)
-        run(3, True)
+        run(*CHUNKS[3], True)
         send(3)
-        combine(s, 1)
+        combine(s, 2)
         to_high.wait_recv()
         halo_planes(0)
         x_pass(s, range(0, 8), range(3, 6), range(3, 6), ((6, 0),), (), True)
-        send(2)
+        send(4)
+        send(5)
         to_low.wait_send()
         to_high.wait_send()
         for copy in y_halo(s):
@@ -441,11 +449,14 @@
         if n_z > 1:
             whole(ar2.at[s], a2s_sem).wait()
         finish(s, 0)
+        finish(s, 1)
         combine(s, 3)
-        finish(s, 1)
-        combine(s, 2)
+        finish(s, 2)
+        combine(s, 4)
+        combine(s, 5)
         finish(s, 3)
-        finish(s, 2)
+        finish(s, 4)
+        finish(s, 5)
         for chunk in range(len(CHUNKS)):
             for h in range(2):
                 swap(s, h, chunk, False).wait_send()
@@ -453,9 +464,8 @@
         return 0
 
     lax.fori_loop(0, SWEEPS, sweep, 0)
-    store = pltpu.make_async_copy(stage, out_hbm.at[0], out_sem)
-    store.start()
-    store.wait()
+    for chunk in range(len(CHUNKS)):
+        store(chunk).wait()
 
 
 def call(sizes, initial, guesses):
@@ -468,7 +478,7 @@
     def vm(*shape):
         return pltpu.VMEM(shape, f32)
 
-    return pl.pallas_call(
+    scaled = pl.pallas_call(
         functools.partial(kernel, sizes),
         out_shape=jax.ShapeDtypeStruct(guesses.shape, f32),
         in_specs=[pl.BlockSpec(memory_space=pl.ANY)] * 2,
@@ -478,8 +488,8 @@
             vm(5, NX + 6, NY, LANES),
             vm(5, NX, 32, LANES),
             vm(5, NX, NY, LANES),
-            vm(2, 5, 40, LANES),
-            vm(5, 24, LANES),
+            vm(2, 8 * 40, LANES),
+            vm(8 * 24, LANES),
             vm(2, 2, 5, *tile),
             vm(2, NX, 5, *tile),
             vm(SWEEPS, 2, NX, 5, *tile),
@@ -496,7 +506,7 @@
             vm(1, LANES),
             vm(SWEEPS, max(n_z - 1, 1), 1, LANES),
             vm(3, *tile),
-            dma((2,)), dma,
+            dma((2,)), dma((chunks,)),
             dma((2,)), dma((SWEEPS, 2)), dma((2,)), dma((SWEEPS, 2)),
             dma, dma((SWEEPS,)), dma, dma((SWEEPS,)),
             dma((2, chunks)), dma((SWEEPS, 2, chunks)), dma((2, chunks)), dma((SWEEPS, 2, chunks)),
@@ -505,6 +515,7 @@
             collective_id=0, has_side_effects=True, vmem_limit_bytes=60 << 20
         ),
     )(initial, guesses)
+    return scaled * (1.0 / SCALE)
 
 
 def solution(mesh):

time: 73.9 us -> 73.6 us (level)
  the two profiles are of different devices: /device:TPU:8 before, /device:TPU:2 now
where the time goes in v3:
time: 73.6 us; the launch traced here: 73.5 us
  Pallas kernels  71.6 us (97%)
  other arithmetic  1.85 us (3%)
    pallas_call x1, Pallas kernels, call(): pl.pallas_call(functools.partial(kernel, sizes), out_shape=jax.ShapeDtype...  71.6 us
    mul x1, other arithmetic, call(): return scaled * (1.0 / SCALE)  1.85 us

profile of v3, /device:TPU:2, one launch (start us, length us, event | category | flops | bytes accessed | tf_op | source)
XLA Modules:
  0.0 73.5 jit_solution(14879511526991718821)
XLA Ops:
  0.0 71.6 %shard_map.28 = f32[1,5,12,16,128]{4,3,2,1,0:T(8,128)} custom-call(f32[5,12,16,128]{3,2,1,0:T(8,128)} %init_hbm.1, f32[1,5,12,16,128]{4,3,2,1,0:T(8,128)} %guess_hbm.1), custom_call_target="tpu_custom_call" | custom-call | tf_op jit(solution)/shard_map/pallas_call | solution.py:481
  71.6 1.9 %broadcast_multiply_fusion = f32[1,5,12,16,128]{4,3,2,1,0:T(8,128)} fusion(f32[1,5,12,16,128]{4,3,2,1,0:T(8,128)} %shard_map.28), kind=kLoop, calls=%fused_computation | loop fusion | flops 122880 | bytes 983040 | tf_op jit(solution)/shard_map/mul | solution.py:518
